TPU v7x, 32 devices: a whole 2x2x4 slice. The times are simulated.
32 devices in a mesh: row: 8 (over y, x, core), col: 4 (over z).
Axes of the slice: x: 2, y: 2, z: 4, core: 2. Of those that a mesh axis runs over, the one named last changes fastest.
Arguments:
- amplitudes: bfloat16 [4096, 4096], P('row', 'col'), may hold values from -0.1875 to 0.1875
- factors: bfloat16 [4096, 2048], P('col', 'row'), may hold values from -0.125 to 0.125
- tile_map: int32 [16, 16], P('row', 'col'), may hold values 0 or 1
- panel_owner: int32 [2], replicated, may hold values from 0 to 3, as said below
Outputs:
- cycle_term: float32 [4096, 4096], P('row', 'col')
Inputs may be any that keep to these rules, and one draw needn't show every extreme that they name: `panel_owner`: the 2 entries are distinct panel indices, and one of them is the last panel.
All inputs are finite; a program needn't handle non-finite values. No bound on the sum of `tile_map` on one device may be relied on, other than what follows from the above.
Results may differ from a plain program's by a relative error of at most 0.0029.
Values may be sent and summed in bfloat16 or wider, within the bound.
A program may use at most 64 MiB of HBM per device.

v0:
```python
import jax
import jax.numpy as jnp
from jax import lax
from jax.sharding import PartitionSpec as P


def spread(block, axis, owner):
    block = jnp.where(lax.axis_index(axis) == owner, block, jnp.zeros_like(block))
    return lax.psum(block, axis)


def keep_tiles(block, tiles):
    rows, cols = tiles.shape
    shaped = block.reshape(rows, block.shape[0] // rows, cols, block.shape[1] // cols)
    keep = tiles.astype(block.dtype)[:, None, :, None]
    return (shaped * keep).reshape(block.shape)


def outer_rows(left, right):
    return lax.dot_general(
        left, right, (((1,), (1,)), ((), ())), preferred_element_type=jnp.float32
    )


def shards(amplitudes, factors, tile_map, panel_owner):
    kept = keep_tiles(amplitudes, tile_map)
    width = factors.shape[0]
    total = jnp.zeros((kept.shape[0], width), jnp.float32)
    column_factors = lax.all_gather(factors, "row", axis=1, tiled=True)
    for step in range(panel_owner.shape[0]):
        owner = panel_owner[step]
        panel = spread(kept, "col", owner)
        owner_slice = spread(factors, "col", owner)
        owner_factors = lax.all_gather(owner_slice, "row", axis=1, tiled=True)
        integrals = outer_rows(owner_factors, column_factors).astype(jnp.bfloat16)
        total = total + jnp.dot(panel, integrals, preferred_element_type=jnp.float32)
    return keep_tiles(total, tile_map)


def solution(mesh):
    in_specs = (P("row", "col"), P("col", "row"), P("row", "col"), P())
    out_specs = P("row", "col")
    return jax.shard_map(shards, mesh=mesh, in_specs=in_specs, out_specs=out_specs, check_vma=False)
```

profile of v0, /device:TPU:0, one launch (start us, length us, event | category | flops | bytes accessed | tf_op | source)
XLA Modules:
  0.0 232.9 jit_solution(12405336362898462879)
XLA Ops:
  7.4 0.0 copy-start
  7.4 0.0 all-reduce.3.cloned.1.call-start
  7.4 0.8 fusion.10
  8.2 1.3 fusion.11
  9.4 0.3 mul.22
  9.8 0.2 copy.5
  11.2 2.1 broadcast_select_fusion.3
  13.3 0.0 copy-done
  13.3 1.5 broadcast_select_fusion.1
  14.8 0.0 all-reduce.3.cloned.1.call-update
  14.9 0.0 all-gather.6.cloned.1.call-start
  14.9 0.5 all-gather.6.cloned.1.call-update
  15.4 0.0 all-gather.8.cloned.1.call-start
  15.5 123.3 %all-reduce.3.cloned.1.call-done = (bf16[512,1024]{1,0:T(8,128)(2,1)}, bf16[1024,256]{1,0:T(8,128)(2,1)}, bf16[512,1024]{1,0:T(8,128)(2,1)}, bf16[1024,256]{1,0:T(8,128)(2,1)}) async-done(((bf16[512,1024]{1,0:T(8,128)(2,1)}, bf16[1024,256]{1,0:T(8,128)(2,1)}, bf16[512,1024]{1,0:T(8,128)(2,1)}, bf16[1024,256]{1,0:T(8,128)(2,1)}), (bf16[512,1024]{1,0:T(8,128)(2,1)}, bf16[1024,256]{1,0:T(8,128)(2,1)}, ...) | async-done | bytes 3145744 | tf_op jit(solution)/shard_map/psum | solution.py:9
  138.8 0.0 all-gather.8.cloned.1.call-update
  138.9 0.0 all-gather.4.cloned.1.call-start
  138.9 0.5 all-gather.4.cloned.1.call-update
  139.4 0.3 mul.25
  139.8 0.5 copy.6
  140.3 0.0 all-gather.6.cloned.1.call-done
  140.3 34.9 %all-gather.8.cloned.1.call-done = bf16[1024,2048]{1,0:T(8,128)(2,1)} async-done(((bf16[1024,256]{1,0:T(8,128)(2,1)}), bf16[1024,2048]{1,0:T(8,128)(2,1)}) %all-gather.8.cloned.1.call-update) | async-done | bytes 4194320 | tf_op jit(solution)/shard_map/all_gather | solution.py:34
  175.2 0.0 copy-start.1
  175.2 10.8 %fusion = f32[512,1024]{1,0:T(8,128)} fusion(bf16[512,1024]{1,0:T(8,128)(2,1)} %get-tuple-element.5, bf16[1024,2048]{1,0:T(8,128)(2,1)} %all-gather.8.cloned.1.call-done, bf16[1024,2048]{1,0:T(8,128)(2,1)} %all-gather.6.cloned.1.call-done), kind=kOutput, calls=%fused_computation.1 | convolution fusion | flops 5369757696 | bytes 11534336 | tf_op jit(solution)/shard_map/dot_general | solution.py:36
  186.0 28.2 %all-gather.4.cloned.1.call-done = bf16[1024,2048]{1,0:T(8,128)(2,1)} async-done(((bf16[1024,256]{1,0:T(8,128)(2,1)}), bf16[1024,2048]{1,0:T(8,128)(2,1)}) %all-gather.4.cloned.1.call-update) | async-done | bytes 4194320 | tf_op jit(solution)/shard_map/all_gather | solution.py:34
  214.2 0.0 copy-done.1
  214.2 11.1 %add_multiply_fusion = f32[512,1024]{1,0:T(8,128)} fusion(f32[512,1024]{1,0:T(8,128)S(1)} %bitcast.17, f32[512,1024]{1,0:T(8,128)} %fusion, bf16[512,1024]{1,0:T(8,128)(2,1)S(1)} %copy-done.1, bf16[1024,2048]{1,0:T(8,128)(2,1)} %all-gather.4.cloned.1.call-done, bf16[1024,2048]{1,0:T(8,128)(2,1)} %all-gather.6.cloned.1.call-done), kind=kOutput, calls=%fused_computation | convolution fusion | flops 5370806272 | bytes 15728640 | tf_op jit(solution)/shard_map/dot_general | solution.py:36
Async XLA Ops:
  7.4 6.0 %copy-start = (bf16[512,1024]{1,0:T(8,128)(2,1)S(1)}, bf16[512,1024]{1,0:T(8,128)(2,1)}, u32[]{:S(2)}) copy-start(bf16[512,1024]{1,0:T(8,128)(2,1)} %param.4) | copy-start | bytes 3145732
  7.4 131.5 %all-reduce.3.cloned.1.call-start = ((), (), s32[]{:S(2)}) async-start(), calls=%async_computation.3 | async-start | bytes 6291456 | tf_op jit(solution)/shard_map/psum | solution.py:9
  14.9 125.4 %all-gather.6.cloned.1.call-start = ((), (), s32[]{:S(2)}) async-start(), calls=%async_computation.1 | async-start | bytes 4718592 | tf_op jit(solution)/shard_map/all_gather | solution.py:29
  15.4 159.8 %all-gather.8.cloned.1.call-start = ((), (), s32[]{:S(2)}) async-start(), calls=%async_computation.2 | async-start | bytes 4718592 | tf_op jit(solution)/shard_map/all_gather | solution.py:34
  138.9 75.3 %all-gather.4.cloned.1.call-start = ((), (), s32[]{:S(2)}) async-start(), calls=%async_computation | async-start | bytes 4718592 | tf_op jit(solution)/shard_map/all_gather | solution.py:34
  175.2 39.0 %copy-start.1 = (bf16[512,1024]{1,0:T(8,128)(2,1)S(1)}, bf16[512,1024]{1,0:T(8,128)(2,1)}, u32[]{:S(2)}) copy-start(bf16[512,1024]{1,0:T(8,128)(2,1)} %get-tuple-element.7) | copy-start | bytes 3145732
Sparse Core Ops, SparseCore 0:
  15.0 123.8 all-reduce.2
Sparse Core Ops, SparseCore 1:
  17.2 39.9 all-gather.5
  139.0 36.2 all-gather.7
  177.0 37.2 all-gather.3
where the time goes:
time: 233 us
  waiting for transfers between devices  188 us (81%)
  matrix products  21.9 us (9%)
  between operations  16.3 us (7%)
  other arithmetic  4.41 us (2%)
  local copies, waits for them, and re-layouts  2.65 us (1%)
    psum x1, waiting for transfers between devices, spread(): return lax.psum(block, axis)  123 us
    all_gather x2, waiting for transfers between devices, shards(): owner_factors = lax.all_gather(owner_slice, 'row', axis=1, tiled=True)  63.1 us
    dot_general x2, matrix products, shards(): jnp.dot(panel, integrals, preferred_element_type=jnp.float32)  21.9 us
  transfers between devices with their start and end apart: 4, of which 3 were waited for; matrix products, arithmetic and copies ran while one was open for 5% of the time, Pallas kernels for 0%

commit v1 on v0

v1 whole, which is shorter than its diff:
```python
import jax
import jax.numpy as jnp
from jax import lax
from jax.sharding import PartitionSpec as P


def keep_tiles(block, tiles):
    rows, cols = tiles.shape
    shaped = block.reshape(rows, block.shape[0] // rows, cols, block.shape[1] // cols)
    keep = tiles.astype(block.dtype)[:, None, :, None]
    return (shaped * keep).reshape(block.shape)


def shards(amplitudes, factors, tile_map, panel_owner):
    mine = jnp.any(panel_owner == lax.axis_index("col"))
    kept = keep_tiles(amplitudes, tile_map * mine.astype(tile_map.dtype))
    column_factors = lax.all_gather(factors, "row", axis=1, tiled=True)
    half = jnp.dot(kept, column_factors, preferred_element_type=jnp.float32)
    half = lax.psum(half.astype(jnp.bfloat16), "col")
    total = lax.dot_general(
        half, column_factors, (((1,), (1,)), ((), ())), preferred_element_type=jnp.float32
    )
    return keep_tiles(total, tile_map)


def solution(mesh):
    in_specs = (P("row", "col"), P("col", "row"), P("row", "col"), P())
    out_specs = P("row", "col")
    return jax.shard_map(shards, mesh=mesh, in_specs=in_specs, out_specs=out_specs, check_vma=False)
```

time: 233 us -> 155 us (0.67)
  waiting for transfers between devices: 188 us -> 125 us
  matrix products: 21.9 us -> 12.4 us
  other arithmetic: 4.41 us -> 2.06 us
    all_gather x2 -> x0, waiting for transfers between devices: 63.1 us -> none  [shards(): owner_factors = lax.all_gather(owner_slice, 'row', axis=1, tiled=True)]
    all_gather x1, waiting for transfers between devices: 0.03 us -> 38.7 us  [shards(): column_factors = lax.all_gather(factors, 'row', axis=1, tiled=True)]
    psum x1, waiting for transfers between devices: 123 us -> 85.5 us  [shards(): half = lax.psum(half.astype(jnp.bfloat16), 'col')]
    dot_general x2, matrix products: 21.9 us -> 12.4 us  [the longest x1 6.51 us: shards(): lax.dot_general(half, column_factors, (((1,), (1,)), ((), ())), preferred...]
    select_n x2 -> x0, other arithmetic: 3.63 us -> none  [spread(): jnp.where(lax.axis_index(axis) == owner, block, jnp.zeros_like(block))]
  transfers between devices with their start and end apart: 4 -> 2, of which waited for: 3 -> 2; matrix products, arithmetic and copies ran while one was open for 5% -> 2% of each run, Pallas kernels for 0% -> 0%
where the time goes in v1:
time: 155 us
  waiting for transfers between devices  125 us (81%)
  between operations  14.1 us (9%)
  matrix products  12.4 us (8%)
  other arithmetic  2.06 us (1%)
    psum x1, waiting for transfers between devices, shards(): half = lax.psum(half.astype(jnp.bfloat16), 'col')  85.5 us
    all_gather x1, waiting for transfers between devices, shards(): column_factors = lax.all_gather(factors, 'row', axis=1, tiled=True)  38.7 us
    dot_general x1, matrix products, shards(): lax.dot_general(half, column_factors, (((1,), (1,)), ((), ())), preferred...  6.51 us
    dot_general x1, matrix products, shards(): half = jnp.dot(kept, column_factors, preferred_element_type=jnp.float32)  5.87 us
  transfers between devices with their start and end apart: 2, of which 2 were waited for; matrix products, arithmetic and copies ran while one was open for 2% of the time, Pallas kernels for 0%

profile of v1, /device:TPU:0, one launch (start us, length us, event | category | flops | bytes accessed | tf_op | source)
XLA Modules:
  0.0 154.8 jit_solution(7773014313803504044)
XLA Ops:
  6.5 0.0 copy-start
  6.5 0.0 all-gather.2.cloned.1.call-start
  6.5 0.7 all-gather.2.cloned.1.call-update
  7.3 0.0 all-reduce.2.cloned.1.call-start
  7.3 1.3 compare_reduce_fusion
  9.3 0.8 multiply_convert_fusion
  10.0 0.3 mul.30
  10.4 0.2 copy.5
  10.6 38.7 %all-gather.2.cloned.1.call-done = bf16[1024,2048]{1,0:T(8,128)(2,1)} async-done(((bf16[1024,256]{1,0:T(8,128)(2,1)}), bf16[1024,2048]{1,0:T(8,128)(2,1)}) %all-gather.2.cloned.1.call-update) | async-done | bytes 4194320 | tf_op jit(solution)/shard_map/all_gather | solution.py:17
  49.3 0.0 copy-done
  49.3 5.9 %convolution_convert_fusion = bf16[512,2048]{1,0:T(8,128)(2,1)} fusion(bf16[1024,2048]{1,0:T(8,128)(2,1)} %all-gather.2.cloned.1.call-done, bf16[512,1024]{1,0:T(8,128)(2,1)S(1)} %copy-done, bf16[512,1024]{1,0:T(8,128)(2,1)S(1)} %bitcast.12), kind=kOutput, calls=%fused_computation | convolution fusion | flops 2149056512 | bytes 8388608 | tf_op jit(solution)/shard_map/dot_general | solution.py:18
  55.2 0.0 all-reduce.2.cloned.1.call-update
  55.2 0.3 mul.33
  55.5 0.5 copy.6
  56.0 85.5 %all-reduce.2.cloned.1.call-done = bf16[512,2048]{1,0:T(8,128)(2,1)} async-done(((bf16[512,2048]{1,0:T(8,128)(2,1)}), bf16[512,2048]{1,0:T(8,128)(2,1)}) %all-reduce.2.cloned.1.call-update) | async-done | bytes 2097168 | tf_op jit(solution)/shard_map/psum | solution.py:19
  141.5 6.5 %convolution_multiply_fusion = f32[512,1024]{1,0:T(8,128)} fusion(f32[512,1024]{1,0:T(8,128)S(1)} %bitcast.11, bf16[512,2048]{1,0:T(8,128)(2,1)} %all-reduce.2.cloned.1.call-done, bf16[1024,2048]{1,0:T(8,128)(2,1)} %all-gather.2.cloned.1.call-done), kind=kOutput, calls=%fused_computation.1 | convolution fusion | flops 2148007936 | bytes 10485760 | tf_op jit(solution)/shard_map/dot_general | solution.py:20
Async XLA Ops:
  6.5 42.8 %copy-start = (bf16[512,1024]{1,0:T(8,128)(2,1)S(1)}, bf16[512,1024]{1,0:T(8,128)(2,1)}, u32[]{:S(2)}) copy-start(bf16[512,1024]{1,0:T(8,128)(2,1)} %param.4) | copy-start | bytes 3145732
  6.5 42.8 %all-gather.2.cloned.1.call-start = ((), (), s32[]{:S(2)}) async-start(), calls=%async_computation | async-start | bytes 4718592 | tf_op jit(solution)/shard_map/all_gather | solution.py:17
  7.3 134.2 %all-reduce.2.cloned.1.call-start = ((), (), s32[]{:S(2)}) async-start(), calls=%async_computation.1 | async-start | bytes 4194304 | tf_op jit(solution)/shard_map/psum | solution.py:19
Sparse Core Ops, SparseCore 0:
  9.2 40.0 all-gather.1
  55.3 86.1 all-reduce.1

commit v2 on v1

v2 whole, which is shorter than its diff:
```python
import functools

import jax
import jax.numpy as jnp
from jax import lax
from jax.experimental import pallas as pl
from jax.experimental.pallas import tpu as pltpu
from jax.sharding import PartitionSpec as P

MESH = pl.DeviceIdType.MESH
SPLITS = 2
SKEW = 2


def flip(index, bits):
    bit = 1
    while bit <= bits:
        if bits & bit:
            index = index + bit - 2 * bit * ((index // bit) % 2)
        bit *= 2
    return index


def keep_tiles(block, tiles):
    rows, cols = tiles.shape
    shaped = block.reshape(rows, block.shape[0] // rows, cols, block.shape[1] // cols)
    keep = tiles.astype(block.dtype)[:, None, :, None]
    return (shaped * keep).reshape(block.shape)


def kernel(
    cols, chips, owner_ref, tiles_ref, amp_ref, own_ref, out_ref,
    held, kept, local, down_out, down_in, up_out, up_in,
    held_send, held_recv, down_send, down_recv, up_send, up_recv,
):
    row, col = lax.axis_index("row"), lax.axis_index("col")
    core, chip = row % 2, row // 2
    partner = row + 1 - 2 * core
    blocks = 2 * chips
    steps = blocks * SPLITS
    height = kept.shape[0] // SPLITS
    first, last = col == 0, col == cols - 1

    barrier = pltpu.get_barrier_semaphore()

    def greet(**where):
        pl.semaphore_signal(barrier, inc=1, device_id=where, device_id_type=MESH)

    greet(row=partner)
    for d in range(1, chips):
        greet(row=2 * flip(chip, d) + core)

    @pl.when(col > 0)
    def _():
        greet(col=col - 1)

    @pl.when(col < cols - 1)
    def _():
        greet(col=col + 1)

    ends = jnp.where(first, 1, 0) + jnp.where(last, 1, 0)
    pl.semaphore_wait(barrier, chips + 2 - ends)

    def to_partner(src, slot):
        return pltpu.make_async_remote_copy(
            src_ref=src, dst_ref=held.at[slot], send_sem=held_send.at[slot],
            recv_sem=held_recv.at[slot], device_id={"row": partner}, device_id_type=MESH,
        )

    def to_chip(d):
        return pltpu.make_async_remote_copy(
            src_ref=own_ref, dst_ref=held.at[2 * d], send_sem=held_send.at[2 * d],
            recv_sem=held_recv.at[2 * d], device_id={"row": 2 * flip(chip, d) + core},
            device_id_type=MESH,
        )

    def down(step):
        return pltpu.make_async_remote_copy(
            src_ref=down_out.at[step], dst_ref=down_in.at[step], send_sem=down_send.at[step],
            recv_sem=down_recv.at[step], device_id={"col": jnp.maximum(col - 1, 0)},
            device_id_type=MESH,
        )

    def up(step):
        return pltpu.make_async_remote_copy(
            src_ref=up_out.at[step], dst_ref=up_in.at[step], send_sem=up_send.at[step],
            recv_sem=up_recv.at[step], device_id={"col": jnp.minimum(col + 1, cols - 1)},
            device_id_type=MESH,
        )

    to_partner(own_ref, 1).start()
    for d in range(1, chips):
        to_chip(d).start()

    owns = jnp.int32(0)
    for s in range(owner_ref.shape[0]):
        owns = owns + jnp.where(owner_ref[s] == col, 1, 0)
    tile_rows, tile_cols = tiles_ref.shape
    th, tw = kept.shape[0] // tile_rows, kept.shape[1] // tile_cols
    for i in range(tile_rows):
        for j in range(tile_cols):
            keep = (tiles_ref[i, j] * owns).astype(jnp.float32)
            part = amp_ref[i * th:(i + 1) * th, j * tw:(j + 1) * tw].astype(jnp.float32)
            kept[i * th:(i + 1) * th, j * tw:(j + 1) * tw] = (part * keep).astype(kept.dtype)
    held[0] = own_ref[...]
    out_ref[...] = jnp.zeros_like(out_ref)

    @pl.when(last)
    def _():
        down_in[...] = jnp.zeros_like(down_in)

    @pl.when(first)
    def _():
        up_in[...] = jnp.zeros_like(up_in)

    def body(i, carry):
        @pl.when(i < steps)
        def _():
            block, part = i // SPLITS, i % SPLITS

            @pl.when((part == 0) & (block > 0))
            def _():
                to_partner(own_ref, block).wait_recv()

                @pl.when(block % 2 == 0)
                def _():
                    to_partner(held.at[block], block + 1).start()

            local[i] = jnp.dot(
                kept[pl.ds(part * height, height), :], held[block],
                preferred_element_type=jnp.float32,
            )

        going_down = i - (cols - 1 - col) * SKEW

        @pl.when((going_down >= 0) & (going_down < steps))
        def _():
            @pl.when(col < cols - 1)
            def _():
                down(going_down).wait_recv()

            @pl.when(col > 0)
            def _():
                value = local[going_down] + down_in[going_down].astype(jnp.float32)
                down_out[going_down] = value.astype(down_out.dtype)
                down(going_down).start()

        going_up = i - col * SKEW

        @pl.when((going_up >= 0) & (going_up < steps))
        def _():
            @pl.when(col > 0)
            def _():
                up(going_up).wait_recv()

            @pl.when(col < cols - 1)
            def _():
                value = local[going_up] + up_in[going_up].astype(jnp.float32)
                up_out[going_up] = value.astype(up_out.dtype)
                up(going_up).start()

        done = i - (cols - 1) * SKEW

        @pl.when(done >= 0)
        def _():
            block, part = done // SPLITS, done % SPLITS
            value = local[done] + down_in[done].astype(jnp.float32) + up_in[done].astype(jnp.float32)
            rows = pl.ds(part * height, height)
            out_ref[rows, :] += lax.dot_general(
                value.astype(held.dtype), held[block], (((1,), (1,)), ((), ())),
                preferred_element_type=jnp.float32,
            )

        return carry

    lax.fori_loop(0, steps + (cols - 1) * SKEW, body, 0)

    for slot in range(1, blocks):
        to_partner(own_ref, slot).wait_send()

    def drain(i, carry):
        @pl.when(col > 0)
        def _():
            down(i).wait_send()

        @pl.when(col < cols - 1)
        def _():
            up(i).wait_send()

        return carry

    lax.fori_loop(0, steps, drain, 0)


def shards(row_count, col_count, amplitudes, factors, tile_map, panel_owner):
    rows, width = amplitudes.shape
    pairs, depth = factors.shape
    chips = row_count // 2
    blocks = row_count
    steps = blocks * SPLITS
    height = rows // SPLITS
    dma = pltpu.SemaphoreType.DMA
    chunk = (steps, height, depth)
    total = pl.pallas_call(
        functools.partial(kernel, col_count, chips),
        out_shape=jax.ShapeDtypeStruct((rows, pairs), jnp.float32),
        in_specs=[pl.BlockSpec(memory_space=pltpu.SMEM)] * 2 + [pl.BlockSpec(memory_space=pltpu.VMEM)] * 2,
        out_specs=pl.BlockSpec(memory_space=pltpu.VMEM),
        scratch_shapes=[
            pltpu.VMEM((blocks, pairs, depth), factors.dtype),
            pltpu.VMEM((rows, width), amplitudes.dtype),
            pltpu.VMEM(chunk, jnp.float32),
        ] + [pltpu.VMEM(chunk, jnp.bfloat16)] * 4 + [
            dma((blocks,)), dma((blocks,)),
            dma((steps,)), dma((steps,)), dma((steps,)), dma((steps,)),
        ],
        compiler_params=pltpu.CompilerParams(collective_id=0, has_side_effects=True),
    )(panel_owner, tile_map, amplitudes, factors)
    return keep_tiles(total, tile_map)


def solution(mesh):
    in_specs = (P("row", "col"), P("col", "row"), P("row", "col"), P())
    out_specs = P("row", "col")
    body = functools.partial(shards, mesh.shape["row"], mesh.shape["col"])
    return jax.shard_map(body, mesh=mesh, in_specs=in_specs, out_specs=out_specs, check_vma=False)
```

time: 155 us -> 71.9 us (0.46)
  waiting for transfers between devices: 125 us -> 0 us
  Pallas kernels: 0 us -> 66.9 us
  between operations: 14.1 us -> 0.02 us
  matrix products: 12.4 us -> 0 us
  other arithmetic: 2.06 us -> 3.98 us
    psum x1 -> x0, waiting for transfers between devices: 85.5 us -> none  [shards(): half = lax.psum(half.astype(jnp.bfloat16), 'col')]
    pallas_call x0 -> x1, Pallas kernels: none -> 66.9 us  [shards(): pl.pallas_call(functools.partial(kernel, col_count, chips), out_shape=jax...]
    all_gather x1 -> x0, waiting for transfers between devices: 38.7 us -> none  [shards(): column_factors = lax.all_gather(factors, 'row', axis=1, tiled=True)]
    dot_general x2 -> x0, matrix products: 12.4 us -> none  [the longest x1 6.51 us: shards(): lax.dot_general(half, column_factors, (((1,), (1,)), ((), ())), preferred...]
    mul x0 -> x1, other arithmetic: none -> 3.3 us  [keep_tiles(): return (shaped * keep).reshape(block.shape)]
  transfers between devices with their start and end apart: 2 -> 0, of which waited for: 2 -> 0; matrix products, arithmetic and copies ran while one was open for 2% -> 0% of each run, Pallas kernels for 0% -> 0%
where the time goes in v2:
time: 71.9 us; the launch traced here: 71.7 us
  Pallas kernels  66.9 us (93%)
  other arithmetic  3.98 us (6%)
  local copies, waits for them, and re-layouts  0.81 us (1%)
    pallas_call x1, Pallas kernels, shards(): pl.pallas_call(functools.partial(kernel, col_count, chips), out_shape=jax...  66.9 us
    mul x1, other arithmetic, keep_tiles(): return (shaped * keep).reshape(block.shape)  3.3 us

profile of v2, /device:TPU:0, one launch (start us, length us, event | category | flops | bytes accessed | tf_op | source)
XLA Modules:
  0.0 71.7 jit_solution(14432762950986524970)
XLA Ops:
  0.0 0.7 convert_element_type.3
  0.7 0.3 mul.11
  1.0 0.5 copy.5
  1.5 66.9 %shard_map.46 = f32[512,1024]{1,0:T(8,128)} custom-call(s32[2]{0:T(128)} %owner_ref.1, s32[2,4]{1,0:T(2,128)} %tiles_ref.1, bf16[512,1024]{1,0:T(8,128)(2,1)} %amp_ref.1, bf16[1024,256]{1,0:T(8,128)(2,1)} %own_ref.1), custom_call_target="tpu_custom_call" | custom-call | tf_op jit(solution)/shard_map/pallas_call | solution.py:204
  68.4 3.3 %mul.13 = f32[512,1024]{1,0:T(8,128)} multiply(f32[512,1024]{1,0:T(8,128)} %shard_map.46, f32[512,1024]{1,0:T(8,128)S(1)} %bitcast.3) | non-fusion elementwise | flops 524288 | bytes 6291456 | tf_op jit(solution)/shard_map/mul | solution.py:28

commit v3 on v2

--- a/solution.py
+++ b/solution.py
@@ -8,8 +8,9 @@
 from jax.sharding import PartitionSpec as P
 
 MESH = pl.DeviceIdType.MESH
-SPLITS = 2
-SKEW = 2
+SPLITS = 4
+SKEW = 3
+GRANT = 62 * 1024 * 1024
 
 
 def flip(index, bits):
@@ -23,9 +24,9 @@
 
 def keep_tiles(block, tiles):
     rows, cols = tiles.shape
-    shaped = block.reshape(rows, block.shape[0] // rows, cols, block.shape[1] // cols)
-    keep = tiles.astype(block.dtype)[:, None, :, None]
-    return (shaped * keep).reshape(block.shape)
+    keep = jnp.repeat(tiles.astype(block.dtype), block.shape[1] // cols, axis=1)
+    shaped = block.reshape(rows, block.shape[0] // rows, block.shape[1])
+    return (shaped * keep[:, None, :]).reshape(block.shape)
 
 
 def kernel(
@@ -58,9 +59,6 @@
     def _():
         greet(col=col + 1)
 
-    ends = jnp.where(first, 1, 0) + jnp.where(last, 1, 0)
-    pl.semaphore_wait(barrier, chips + 2 - ends)
-
     def to_partner(src, slot):
         return pltpu.make_async_remote_copy(
             src_ref=src, dst_ref=held.at[slot], send_sem=held_send.at[slot],
@@ -75,22 +73,20 @@
         )
 
     def down(step):
-        return pltpu.make_async_remote_copy(
-            src_ref=down_out.at[step], dst_ref=down_in.at[step], send_sem=down_send.at[step],
+        block, rows = chunk_of(step)
+        return pltpu.make_async_remote_copy(
+            src_ref=down_out.at[block, rows, :], dst_ref=down_in.at[block, rows, :], send_sem=down_send.at[step],
             recv_sem=down_recv.at[step], device_id={"col": jnp.maximum(col - 1, 0)},
             device_id_type=MESH,
         )
 
     def up(step):
-        return pltpu.make_async_remote_copy(
-            src_ref=up_out.at[step], dst_ref=up_in.at[step], send_sem=up_send.at[step],
+        block, rows = chunk_of(step)
+        return pltpu.make_async_remote_copy(
+            src_ref=up_out.at[block, rows, :], dst_ref=up_in.at[block, rows, :], send_sem=up_send.at[step],
             recv_sem=up_recv.at[step], device_id={"col": jnp.minimum(col + 1, cols - 1)},
             device_id_type=MESH,
         )
-
-    to_partner(own_ref, 1).start()
-    for d in range(1, chips):
-        to_chip(d).start()
 
     owns = jnp.int32(0)
     for s in range(owner_ref.shape[0]):
@@ -103,22 +99,26 @@
             part = amp_ref[i * th:(i + 1) * th, j * tw:(j + 1) * tw].astype(jnp.float32)
             kept[i * th:(i + 1) * th, j * tw:(j + 1) * tw] = (part * keep).astype(kept.dtype)
     held[0] = own_ref[...]
-    out_ref[...] = jnp.zeros_like(out_ref)
-
-    @pl.when(last)
-    def _():
-        down_in[...] = jnp.zeros_like(down_in)
-
-    @pl.when(first)
-    def _():
-        up_in[...] = jnp.zeros_like(up_in)
+
+    ends = jnp.where(first, 1, 0) + jnp.where(last, 1, 0)
+    pl.semaphore_wait(barrier, chips + 2 - ends)
+    to_partner(own_ref, 1).start()
+    for d in range(1, chips):
+        to_chip(d).start()
+
+    def chunk_of(step):
+        return step // SPLITS, pl.ds(pl.multiple_of(step % SPLITS * height, height), height)
+
+    near = jnp.minimum(col, cols - 1 - col)
 
     def body(i, carry):
-        @pl.when(i < steps)
-        def _():
-            block, part = i // SPLITS, i % SPLITS
-
-            @pl.when((part == 0) & (block > 0))
+        made = i - near * SKEW
+
+        @pl.when((made >= 0) & (made < steps) & (made % SPLITS == 0))
+        def _():
+            block = made // SPLITS
+
+            @pl.when(block > 0)
             def _():
                 to_partner(own_ref, block).wait_recv()
 
@@ -126,50 +126,66 @@
                 def _():
                     to_partner(held.at[block], block + 1).start()
 
-            local[i] = jnp.dot(
-                kept[pl.ds(part * height, height), :], held[block],
-                preferred_element_type=jnp.float32,
-            )
+            local[block] = jnp.dot(kept[...], held[block], preferred_element_type=jnp.float32)
 
         going_down = i - (cols - 1 - col) * SKEW
 
         @pl.when((going_down >= 0) & (going_down < steps))
         def _():
+            block, rows = chunk_of(going_down)
+
+            @pl.when(last)
+            def _():
+                down_in[block, rows, :] = jnp.zeros((height, down_in.shape[2]), down_in.dtype)
+
             @pl.when(col < cols - 1)
             def _():
                 down(going_down).wait_recv()
 
             @pl.when(col > 0)
             def _():
-                value = local[going_down] + down_in[going_down].astype(jnp.float32)
-                down_out[going_down] = value.astype(down_out.dtype)
+                value = local[block, rows, :] + down_in[block, rows, :].astype(jnp.float32)
+                down_out[block, rows, :] = value.astype(down_out.dtype)
                 down(going_down).start()
 
         going_up = i - col * SKEW
 
         @pl.when((going_up >= 0) & (going_up < steps))
         def _():
+            block, rows = chunk_of(going_up)
+
+            @pl.when(first)
+            def _():
+                up_in[block, rows, :] = jnp.zeros((height, up_in.shape[2]), up_in.dtype)
+
             @pl.when(col > 0)
             def _():
                 up(going_up).wait_recv()
 
             @pl.when(col < cols - 1)
             def _():
-                value = local[going_up] + up_in[going_up].astype(jnp.float32)
-                up_out[going_up] = value.astype(up_out.dtype)
+                value = local[block, rows, :] + up_in[block, rows, :].astype(jnp.float32)
+                up_out[block, rows, :] = value.astype(up_out.dtype)
                 up(going_up).start()
 
         done = i - (cols - 1) * SKEW
 
-        @pl.when(done >= 0)
-        def _():
-            block, part = done // SPLITS, done % SPLITS
-            value = local[done] + down_in[done].astype(jnp.float32) + up_in[done].astype(jnp.float32)
-            rows = pl.ds(part * height, height)
-            out_ref[rows, :] += lax.dot_general(
+        @pl.when((done >= 0) & (done % SPLITS == SPLITS - 1))
+        def _():
+            block = done // SPLITS
+            value = local[block] + down_in[block].astype(jnp.float32) + up_in[block].astype(jnp.float32)
+            product = lax.dot_general(
                 value.astype(held.dtype), held[block], (((1,), (1,)), ((), ())),
                 preferred_element_type=jnp.float32,
             )
+
+            @pl.when(block == 0)
+            def _():
+                out_ref[...] = product
+
+            @pl.when(block > 0)
+            def _():
+                out_ref[...] += product
 
         return carry
 
@@ -198,9 +214,8 @@
     chips = row_count // 2
     blocks = row_count
     steps = blocks * SPLITS
-    height = rows // SPLITS
     dma = pltpu.SemaphoreType.DMA
-    chunk = (steps, height, depth)
+    chunk = (blocks, rows, depth)
     total = pl.pallas_call(
         functools.partial(kernel, col_count, chips),
         out_shape=jax.ShapeDtypeStruct((rows, pairs), jnp.float32),
@@ -214,7 +229,7 @@
             dma((blocks,)), dma((blocks,)),
             dma((steps,)), dma((steps,)), dma((steps,)), dma((steps,)),
         ],
-        compiler_params=pltpu.CompilerParams(collective_id=0, has_side_effects=True),
+        compiler_params=pltpu.CompilerParams(collective_id=0, has_side_effects=True, vmem_limit_bytes=GRANT),
     )(panel_owner, tile_map, amplitudes, factors)
     return keep_tiles(total, tile_map)
 

time: 71.9 us -> 69 us (0.960)
  Pallas kernels: 66.9 us -> 64.8 us
  local copies, waits for them, and re-layouts: 0.81 us -> 0.08 us
    pallas_call x1, Pallas kernels: 66.9 us -> 64.8 us  [shards(): pl.pallas_call(functools.partial(kernel, col_count, chips), out_shape=jax...]
where the time goes in v3:
time: 69 us; the launch traced here: 68.8 us
  Pallas kernels  64.8 us (94%)
  other arithmetic  3.95 us (6%)
    pallas_call x1, Pallas kernels, shards(): pl.pallas_call(functools.partial(kernel, col_count, chips), out_shape=jax...  64.8 us
    mul x1, other arithmetic, keep_tiles(): return (shaped * keep[:, None, :]).reshape(block.shape)  3.27 us

profile of v3, /device:TPU:0, one launch (start us, length us, event | category | flops | bytes accessed | tf_op | source)
XLA Modules:
  0.0 68.8 jit_solution(17039987296275977643)
XLA Ops:
  0.0 0.7 convert_element_type.3
  0.7 0.1 broadcast_bitcast_fusion
  0.8 64.8 %shard_map.46 = f32[512,1024]{1,0:T(8,128)} custom-call(s32[2]{0:T(128)} %owner_ref.1, s32[2,4]{1,0:T(2,128)} %tiles_ref.1, bf16[512,1024]{1,0:T(8,128)(2,1)} %amp_ref.1, bf16[1024,256]{1,0:T(8,128)(2,1)} %own_ref.1), custom_call_target="tpu_custom_call" | custom-call | tf_op jit(solution)/shard_map/pallas_call | solution.py:219
  65.6 3.3 %bitcast_multiply_fusion = f32[512,1024]{1,0:T(8,128)} fusion(f32[512,1024]{1,0:T(8,128)} %shard_map.46, f32[2,1024]{1,0:T(2,128)S(1)} %bitcast.5), kind=kLoop, calls=%fused_computation | loop fusion | flops 524288 | bytes 4202496 | tf_op jit(solution)/shard_map/mul | solution.py:29
  (1 shorter events, 0.0 us)

commit v4 on v3

--- a/solution.py
+++ b/solution.py
@@ -10,7 +10,7 @@
 MESH = pl.DeviceIdType.MESH
 SPLITS = 4
 SKEW = 3
-GRANT = 62 * 1024 * 1024
+GRANT = 62390272
 
 
 def flip(index, bits):
@@ -218,7 +218,7 @@
     chunk = (blocks, rows, depth)
     total = pl.pallas_call(
         functools.partial(kernel, col_count, chips),
-        out_shape=jax.ShapeDtypeStruct((rows, pairs), jnp.float32),
+        out_shape=pltpu.VMEM((rows, pairs), jnp.float32),
         in_specs=[pl.BlockSpec(memory_space=pltpu.SMEM)] * 2 + [pl.BlockSpec(memory_space=pltpu.VMEM)] * 2,
         out_specs=pl.BlockSpec(memory_space=pltpu.VMEM),
         scratch_shapes=[

time: 69 us -> 66.1 us (0.958)
  other arithmetic: 3.95 us -> 2.36 us
  Pallas kernels: 64.8 us -> 63.4 us
    mul x1, other arithmetic: 3.27 us -> 1.68 us  [keep_tiles(): return (shaped * keep[:, None, :]).reshape(block.shape)]
    pallas_call x1, Pallas kernels: 64.8 us -> 63.4 us  [shards(): pl.pallas_call(functools.partial(kernel, col_count, chips), out_shape=plt...]
where the time goes in v4:
time: 66.1 us; the launch traced here: 65.9 us
  Pallas kernels  63.4 us (96%)
  other arithmetic  2.36 us (4%)
    pallas_call x1, Pallas kernels, shards(): pl.pallas_call(functools.partial(kernel, col_count, chips), out_shape=plt...  63.4 us
    mul x1, other arithmetic, keep_tiles(): return (shaped * keep[:, None, :]).reshape(block.shape)  1.68 us

profile of v4, /device:TPU:0, one launch (start us, length us, event | category | flops | bytes accessed | tf_op | source)
XLA Modules:
  0.0 65.9 jit_solution(5594722548107741731)
XLA Ops:
  0.0 0.7 %convert_element_type.3 = f32[2,4]{1,0:T(2,128)S(1)} convert(s32[2,4]{1,0:T(2,128)} %tiles_ref.1) | non-fusion elementwise | flops 8 | bytes 64 | tf_op jit(solution)/shard_map/convert_element_type | solution.py:27
  0.7 0.1 broadcast_bitcast_fusion
  0.8 63.4 %shard_map.46 = f32[512,1024]{1,0:T(8,128)S(1)} custom-call(s32[2]{0:T(128)} %owner_ref.1, s32[2,4]{1,0:T(2,128)} %tiles_ref.1, bf16[512,1024]{1,0:T(8,128)(2,1)} %amp_ref.1, bf16[1024,256]{1,0:T(8,128)(2,1)} %own_ref.1), custom_call_target="tpu_custom_call" | custom-call | tf_op jit(solution)/shard_map/pallas_call | solution.py:219
  64.2 1.7 %bitcast_multiply_fusion = f32[512,1024]{1,0:T(8,128)} fusion(f32[512,1024]{1,0:T(8,128)S(1)} %shard_map.46, f32[2,1024]{1,0:T(2,128)S(1)} %bitcast.5), kind=kLoop, calls=%fused_computation | loop fusion | flops 524288 | bytes 4202496 | tf_op jit(solution)/shard_map/mul | solution.py:29
  (1 shorter events, 0.0 us)
